TPU v7x, 512 devices: a whole 4x8x8 slice. The times are simulated.
512 devices in a mesh: section: 2 (over core), sy: 8 (over y), sx: 8 (over z), mb: 4 (over x).
Axes of the slice: x: 4, y: 8, z: 8, core: 2. Of those that a mesh axis runs over, the one named last changes fastest.
Arguments:
- frames: bfloat16 [4, 512, 512, 128], P('mb', 'sy', 'sx'), may hold values from -6 to 6
- encode_weight: bfloat16 [512, 384], replicated, may hold values from -0.25 to 0.25
- conv_weight: bfloat16 [2, 1, 3456, 384], P('section', None, ('sy', 'sx')), may hold values from -0.109375 to 0.109375
- norm_gain: float32 [2, 1, 384], P('section'), may hold values from 0.1 to 1.9
- head_weight: bfloat16 [384, 256], replicated, may hold values from -0.3125 to 0.3125
- prior_logits: bfloat16 [4, 256, 256, 256], P('mb', 'sy', 'sx'), may hold values from -12 to 249
- target_bins: int32 [4, 256, 256], P('mb', 'sy', 'sx'), may hold values from 0 to 255
Outputs:
- section_features: bfloat16 [2, 4, 256, 256, 384], P('section', 'mb', 'sy', 'sx')
- head_step: float32 [384, 256], P('section')
- mean_loss: float32 [], replicated
All inputs are finite; a program needn't handle non-finite values.
Results may differ from a plain program's by a relative error of at most 0.008.
Values may be sent and summed in bfloat16 or wider, within the bound.
No kernel may reach another device: no remote copies, remote signals or barrier semaphores. Data moves between devices by JAX's collectives and lax.ppermute only.
A program may use at most 64 MiB of HBM per device.

v0:
```python
import jax
import jax.numpy as jnp
from jax import lax
from jax.sharding import PartitionSpec as P

FIRST_DILATION = 1


def padded_2(block, sides, width):
    for axis, dim in sides:
        count = lax.axis_size(axis)
        forward = [(i, i + 1) for i in range(count - 1)]
        backward = [(target, source) for source, target in forward]
        low = lax.ppermute(
            lax.slice_in_dim(block, block.shape[dim] - width, None, axis=dim), axis, forward
        )
        high = lax.ppermute(lax.slice_in_dim(block, 0, width, axis=dim), axis, backward)
        block = jnp.concatenate([low, block, high], axis=dim)
    return block


def from_behind(block, axis, distance):
    devices = range(lax.axis_size(axis))
    route = [(i - distance, i) for i in devices if i - distance in devices]
    return lax.ppermute(block, axis, route)


def norm_gelu(activations, gain):
    values = activations.astype(jnp.float32)
    center = jnp.mean(values, axis=-1, keepdims=True)
    offset = values - center
    spread = jnp.mean(offset * offset, axis=-1, keepdims=True)
    normed = offset * lax.rsqrt(spread + 1e-05) * gain
    return jax.nn.gelu(normed, approximate=False).astype(jnp.bfloat16)


def per_device(
    frames, encode_weight, conv_weight, norm_gain, head_weight, prior_logits, target_bins
):
    first_section = lax.axis_index("section") == 0
    micro_count = frames.shape[0]
    side_cells = frames.shape[1] // 2
    input_width = frames.shape[3]
    channels = encode_weight.shape[1]
    bins_count = head_weight.shape[1]
    parts_y = lax.axis_size("sy")
    parts_x = lax.axis_size("sx")
    cell_count = side_cells * side_cells
    kernel = encode_weight.reshape(2, 2, input_width, channels)
    grad_total = jnp.zeros((channels, bins_count), jnp.float32)
    loss_total = jnp.zeros((), jnp.float32)
    first_out = []
    second_out = []
    handed = None
    for tick_index in range(micro_count + 1):
        if tick_index == 0:
            blocks = frames[0].reshape(side_cells, 2, side_cells, 2, input_width)
            activations = jnp.einsum(
                "apbqc,pqco->abo", blocks, kernel, preferred_element_type=jnp.float32
            ).astype(jnp.bfloat16)
        else:
            activations = handed
        apply_reach = FIRST_DILATION * 2**0
        hidden = norm_gelu(activations, norm_gain[0, 0])
        haloed = padded_2(hidden, (("sy", 0), ("sx", 1)), apply_reach)
        zero_padded = jnp.pad(
            hidden, ((apply_reach, apply_reach), (apply_reach, apply_reach), (0, 0))
        )
        apply_padded = jnp.where(first_section, haloed, zero_padded)
        windows = [
            apply_padded[
                tap_row * apply_reach : tap_row * apply_reach + side_cells,
                tap_column * apply_reach : tap_column * apply_reach + side_cells,
            ]
            for tap_row in range(3)
            for tap_column in range(3)
        ]
        patches = jnp.concatenate(windows, axis=2).reshape(cell_count, 9 * channels)
        summed = jnp.dot(
            patches,
            lax.all_gather(conv_weight[0, 0], ("sy", "sx"), axis=0, tiled=True),
            preferred_element_type=jnp.float32,
        )
        activations = (
            activations.astype(jnp.float32) + summed.reshape(side_cells, side_cells, channels)
        ).astype(jnp.bfloat16)
        if tick_index < micro_count:
            first_out.append(activations)
        rows_y = side_cells // parts_y
        rows_x = side_cells // parts_x
        plain_view = activations.reshape(parts_y, rows_y, parts_x, rows_x, channels)
        spaced = activations.reshape(rows_y, parts_y, rows_x, parts_x, channels).transpose(
            1, 0, 3, 2, 4
        )
        outgoing = jnp.where(first_section, spaced, plain_view)
        arrived = lax.all_to_all(
            lax.all_to_all(outgoing, "sy", split_axis=0, concat_axis=0, tiled=True),
            "sx",
            split_axis=2,
            concat_axis=2,
            tiled=True,
        )
        direct = arrived.reshape(side_cells, side_cells, channels)
        restored = arrived.transpose(1, 0, 3, 2, 4).reshape(side_cells, side_cells, channels)
        moved = jnp.where(first_section, direct, restored)
        if tick_index >= 1:
            second_out.append(moved)
            flat_rows = moved.reshape(cell_count, channels)
            logits = jnp.dot(flat_rows, head_weight, preferred_element_type=jnp.float32)
            logits = logits + prior_logits[tick_index - 1].reshape(cell_count, bins_count).astype(
                jnp.float32
            )
            row_top = jnp.max(logits, axis=1, keepdims=True)
            shifted = logits - row_top
            exp_terms = jnp.exp(shifted)
            exp_total = jnp.sum(exp_terms, axis=1, keepdims=True)
            softmax_rows = exp_terms / exp_total
            onehot = (
                target_bins[tick_index - 1].reshape(cell_count, 1)
                == lax.broadcasted_iota(jnp.int32, (1, bins_count), 1)
            ).astype(jnp.float32)
            loss_sum = jnp.sum(jnp.log(exp_total[:, 0]) - jnp.sum(shifted * onehot, axis=1))
            delta_rows = (softmax_rows - onehot).astype(jnp.bfloat16)
            grad_part = lax.dot_general(
                flat_rows, delta_rows, (((0,), (0,)), ((), ())), preferred_element_type=jnp.float32
            )
            grad_part, loss_sum = (grad_part, loss_sum)
            grad_total = jnp.where(first_section, 0.0, grad_part)
            loss_total = jnp.where(first_section, 0.0, loss_sum)
        if tick_index < micro_count:
            handed = from_behind(moved, "section", 1)
    stacked = jnp.stack([jnp.where(first_section, first_out[0], second_out[0])])[None]
    gradient, loss_all = lax.psum((grad_total, loss_total), ("sy", "sx", "mb"))
    head_full = gradient * lax.rsqrt(jnp.mean(gradient * gradient) + 1e-06)
    mean_local = loss_all / (micro_count * lax.axis_size("mb") * cell_count * parts_y * parts_x)
    half_rows = channels // 2
    sent_rows, sent_loss = (
        from_behind(head_full[:half_rows].astype(jnp.bfloat16), "section", -1).astype(jnp.float32),
        from_behind(mean_local.astype(jnp.bfloat16), "section", -1).astype(mean_local.dtype),
    )
    head_step = jnp.where(first_section, sent_rows, head_full[half_rows:])
    mean_loss = jnp.where(first_section, sent_loss, mean_local)
    return (stacked, head_step, mean_loss)


def solution(mesh):
    placed = (
        P("mb", "sy", "sx", None),
        P(),
        P("section", None, ("sy", "sx"), None),
        P("section", None, None),
        P(),
        P("mb", "sy", "sx", None),
        P("mb", "sy", "sx"),
    )
    return jax.shard_map(
        per_device,
        mesh=mesh,
        in_specs=placed,
        out_specs=(P("section", "mb", "sy", "sx", None), P("section", None), P()),
        check_vma=False,
    )
```

profile of v0, /device:TPU:1, one launch (start us, length us, event | category | flops | bytes accessed | tf_op | source)
XLA Modules:
  0.0 957.4 jit_solution(2720262242174057233)
XLA Ops:
  7.2 1.5 copy.50
  8.8 0.7 reduce
  9.5 2.0 convert_reduce_fusion.1
  11.5 0.5 fusion.15
  12.0 3.8 fusion.20
  15.9 4.0 collective-permute-start
  19.9 1.3 collective-permute-start.1
  21.2 3.3 collective-permute-done.1
  24.6 4.0 collective-permute-start.2
  28.6 1.3 collective-permute-start.3
  29.9 4.2 collective-permute-done.3
  34.1 0.6 maximum_select_fusion
  34.7 1.0 slice_dynamic-update-slice_fusion.17
  35.7 1.3 slice_dynamic-update-slice_fusion.16
  37.0 1.3 slice_dynamic-update-slice_fusion.15
  38.3 1.0 slice_dynamic-update-slice_fusion.14
  39.3 1.3 slice_dynamic-update-slice_fusion.13
  40.6 1.3 slice_dynamic-update-slice_fusion.12
  41.9 1.0 slice_dynamic-update-slice_fusion.11
  42.9 1.4 slice_dynamic-update-slice_fusion.10
  44.3 1.3 slice_dynamic-update-slice_fusion.9
  45.5 57.8 %all-gather.3.cloned.1.call-done = bf16[1,1,3456,384]{3,1,0,2:T(2,128)(2,1)} async-done(((bf16[1,1,54,384]{3,1,0,2:T(2,128)(2,1)}), bf16[1,1,3456,384]{3,1,0,2:T(2,128)(2,1)}) %all-gather.3.cloned.1.call-update) | async-done | bytes 2654224 | tf_op jit(solution)/shard_map/all_gather | solution.py:81
  103.3 8.4 fusion.22
  111.9 0.5 bitcast_select_fusion.2
  112.4 23.7 %all_to_all.20 = bf16[8,4,8,4,384]{4,3,1,2,0:T(4,128)(2,1)S(1)} all-to-all(bf16[8,4,8,4,384]{4,3,1,2,0:T(4,128)(2,1)S(1)} %bitcast_select_fusion.2), channel_id=1, replica_groups=mesh['section'=2,'sy'=8,'sx'=8,'mb'=4] {'sy'}, dimensions={0} | all-to-all | bytes 1572864 | tf_op jit(solution)/shard_map/all_to_all | solution.py:97
  136.3 19.7 %all_to_all.21 = bf16[8,4,8,4,384]{4,3,1,0,2:T(4,128)(2,1)S(1)} all-to-all(bf16[8,4,8,4,384]{4,3,1,0,2:T(4,128)(2,1)S(1)} %copy.53), channel_id=1, replica_groups=mesh['section'=2,'sy'=8,'sx'=8,'mb'=4] {'sx'}, dimensions={2} | all-to-all | bytes 1572864 | tf_op jit(solution)/shard_map/all_to_all | solution.py:96
  156.5 0.7 copy.55
  157.3 1.5 collective-permute-start.4
  158.8 9.2 collective-permute-done.4
  168.3 0.5 fusion.8
  168.8 3.8 fusion.13
  172.6 1.4 collective-permute-start.5
  174.0 1.3 collective-permute-start.6
  175.3 3.3 collective-permute-done.6
  178.7 2.2 collective-permute-start.7
  180.9 1.3 collective-permute-start.8
  182.2 3.6 collective-permute-done.8
  185.7 0.6 maximum_select_fusion.1
  186.4 0.4 slice_dynamic-update-slice_fusion.7
  186.8 0.4 slice_dynamic-update-slice_fusion.6
  188.3 0.4 slice_dynamic-update-slice_fusion.1
  188.7 0.4 slice_dynamic-update-slice_fusion
  189.1 3.9 fusion.24
  193.2 0.4 bitcast_select_fusion.1
  193.6 24.2 %all_to_all.22 = bf16[8,4,8,4,384]{4,3,1,2,0:T(4,128)(2,1)S(1)} all-to-all(bf16[8,4,8,4,384]{4,3,1,2,0:T(4,128)(2,1)S(1)} %bitcast_select_fusion.1), channel_id=1, replica_groups=mesh['section'=2,'sy'=8,'sx'=8,'mb'=4] {'sy'}, dimensions={0} | all-to-all | bytes 1572864 | tf_op jit(solution)/shard_map/all_to_all | solution.py:97
  217.8 1.2 copy.58
  219.0 3.5 all-to-all-start.3
  222.9 1.3 copy.63
  224.3 0.8 eq.19
  225.1 16.5 %all-to-all-done.3 = bf16[8,4,8,4,384]{4,3,1,0,2:T(4,128)(2,1)S(1)} async-done(((bf16[8,4,8,4,384]{4,3,1,0,2:T(4,128)(2,1)}), bf16[8,4,8,4,384]{4,3,1,0,2:T(4,128)(2,1)S(1)}, u32[]{:S(2)}, u32[]{:S(2)}) %all-to-all-start.3) | async-done | bytes 786464 | tf_op jit(solution)/shard_map/all_to_all | solution.py:96
  241.9 1.1 reshape.86
  243.0 0.7 copy.60
  243.7 0.4 copy-done.2
  244.3 1.0 copy-done.1
  245.3 0.5 fusion.58
  246.1 1.3 convolution_select_fusion
  247.4 0.6 subtract_reduce_fusion
  248.7 575.3 %psum.15 = f32[]{:T(128)} all-reduce(f32[]{:T(128)S(6)} %select_n.85), channel_id=1, replica_groups=mesh['section'=2,'sy'=8,'sx'=8,'mb'=4] {'sy','sx','mb'}, use_global_device_ids=true, to_apply=%region_10.11 | all-reduce | flops 1 | bytes 8 | tf_op jit(solution)/shard_map/psum | solution.py:133
  824.8 117.5 %collective-permute-start.10 = (bf16[]{:T(256)}, bf16[]{:T(256)}, u32[]{:S(2)}, u32[]{:S(2)}) collective-permute-start(bf16[]{:T(256)} %convert_element_type.60), channel_id=1, source_target_pairs={{256,0},{257,1},{258,2},{259,3},{260,4},{261,5},{262,6},{263,7},{2... | collective-permute-start | bytes 14 | tf_op jit(solution)/shard_map/ppermute | solution.py:25
  942.3 1.7 multiply_reduce_fusion
  944.7 1.0 broadcast_multiply_fusion
  945.7 1.3 collective-permute-start.9
  947.0 1.0 select_bitcast_fusion
  948.7 0.7 slice_select_fusion
  (50 shorter events, 4.2 us)
Async XLA Ops:
  7.2 2.3 copy-start
  7.2 96.1 %all-gather.3.cloned.1.call-start = ((), (), s32[]{:S(2)}) async-start(), calls=%async_computation.5 | async-start | bytes 5391360 | tf_op jit(solution)/shard_map/all_gather | solution.py:81
  15.9 5.3 collective-permute-start
  19.9 4.6 collective-permute-start.1
  24.6 5.3 collective-permute-start.2
  28.6 5.5 collective-permute-start.3
  157.3 10.7 %collective-permute-start.4 = (bf16[32,32,384]{2,1,0:T(8,128)(2,1)S(1)}, bf16[32,32,384]{2,1,0:T(8,128)(2,1)S(1)}, u32[]{:S(2)}, u32[]{:S(2)}) collective-permute-start(bf16[32,32,384]{2,1,0:T(8,128)(2,1)S(1)} %broadcast_select_fusion), channel_id=1, source_target_pairs={{0,256},{1,257},{2,258},{3,259},{4,260},{5,261},{6,262},{7,263},{8... | collective-permute-start | bytes 2359304 | tf_op jit(solution)/shard_map/ppermute | solution.py:25
  172.6 2.7 collective-permute-start.5
  174.0 4.6 collective-permute-start.6
  178.7 3.5 collective-permute-start.7
  180.9 4.9 collective-permute-start.8
  186.3 2.8 slice-start
  187.4 1.7 slice-start.1
  217.8 5.0 copy-start.3
  219.0 22.6 %all-to-all-start.3 = ((bf16[8,4,8,4,384]{4,3,1,0,2:T(4,128)(2,1)}), bf16[8,4,8,4,384]{4,3,1,0,2:T(4,128)(2,1)S(1)}, u32[]{:S(2)}, u32[]{:S(2)}) async-start(bf16[8,4,8,4,384]{4,3,1,0,2:T(4,128)(2,1)} %copy.58), calls=%async_computation.3 | async-start | bytes 1572864 | tf_op jit(solution)/shard_map/all_to_all | solution.py:96
  222.5 719.8 %all-reduce.4.cloned.1.call-start = ((), (), s32[]{:S(2)}) async-start(), calls=%async_computation.4 | async-start | bytes 786432 | tf_op jit(solution)/shard_map/psum | solution.py:133
  243.0 1.1 copy-start.2
  244.1 1.2 copy-start.1
  244.1 1.2 copy-start.4
  824.8 123.2 %collective-permute-start.10 = (bf16[]{:T(256)}, bf16[]{:T(256)}, u32[]{:S(2)}, u32[]{:S(2)}) collective-permute-start(bf16[]{:T(256)} %convert_element_type.60), channel_id=1, source_target_pairs={{256,0},{257,1},{258,2},{259,3},{260,4},{261,5},{262,6},{263,7},{2... | collective-permute-start | bytes 14 | tf_op jit(solution)/shard_map/ppermute | solution.py:25
  945.7 2.9 collective-permute-start.9
Sparse Core Ops, SparseCore 0:
  11.7 91.6 all-gather.2
  247.5 225.9 all-reduce.3
where the time goes:
time: 958 us; the launch traced here: 957 us
  blocking collectives  643 us (67%)
  starting transfers between devices  141 us (15%)
  waiting for transfers between devices  97.9 us (10%)
  local copies, waits for them, and re-layouts  24 us (3%)
  between operations  18.2 us (2%)
  other arithmetic  17.5 us (2%)
  matrix products  16.1 us (2%)
    psum x1, blocking collectives, per_device(): gradient, loss_all = lax.psum((grad_total, loss_total), ('sy', 'sx', 'mb'))  575 us
    ppermute x3, starting transfers between devices, from_behind(): return lax.ppermute(block, axis, route)  120 us
    all_gather x1, waiting for transfers between devices, per_device(): lax.all_gather(conv_weight[0, 0], ('sy', 'sx'), axis=0, tiled=True)  57.8 us
    all_to_all x2, blocking collectives, per_device(): lax.all_to_all(outgoing, 'sy', split_axis=0, concat_axis=0, tiled=True)  47.8 us
    all_to_all x1, blocking collectives, per_device(): lax.all_to_all(lax.all_to_all(outgoing, 'sy', split_axis=0, concat_axis=0...  19.7 us
  transfers between devices with their start and end apart: 14, of which 7 were waited for; matrix products, arithmetic and copies ran while one was open for 3% of the time, Pallas kernels for 0%

commit v1 on v0

--- a/solution.py
+++ b/solution.py
@@ -130,7 +130,10 @@
         if tick_index < micro_count:
             handed = from_behind(moved, "section", 1)
     stacked = jnp.stack([jnp.where(first_section, first_out[0], second_out[0])])[None]
-    gradient, loss_all = lax.psum((grad_total, loss_total), ("sy", "sx", "mb"))
+    quotas_prepare = lambda local_block, named_axis, row_axis: lax.psum(
+        lax.psum(local_block, named_axis), row_axis
+    )
+    gradient, loss_all = quotas_prepare((grad_total, loss_total), "sy", row_axis=("sx", "mb"))
     head_full = gradient * lax.rsqrt(jnp.mean(gradient * gradient) + 1e-06)
     mean_local = loss_all / (micro_count * lax.axis_size("mb") * cell_count * parts_y * parts_x)
     half_rows = channels // 2

time: 958 us -> 500 us (0.52)
  blocking collectives: 643 us -> 143 us
  waiting for transfers between devices: 97.9 us -> 224 us
  starting transfers between devices: 141 us -> 55.1 us
    psum x1 -> x2, blocking collectives: 575 us -> 75.4 us  [the longest x1 62.2 us: per_device(): lax.psum(lax.psum(local_block, named_axis), row_axis)]
    psum x1 -> x2, waiting for transfers between devices: 0.01 us -> 128 us  [the longest x1 71.4 us: per_device(): lax.psum(local_block, named_axis)]
    ppermute x3, starting transfers between devices: 120 us -> 34.4 us  [from_behind(): return lax.ppermute(block, axis, route)]
  transfers between devices with their start and end apart: 14 -> 15, of which waited for: 7 -> 9; matrix products, arithmetic and copies ran while one was open for 3% -> 5% of each run, Pallas kernels for 0% -> 0%
where the time goes in v1:
time: 500 us; the launch traced here: 499 us
  waiting for transfers between devices  224 us (45%)
  blocking collectives  143 us (29%)
  starting transfers between devices  55.1 us (11%)
  local copies, waits for them, and re-layouts  24.6 us (5%)
  other arithmetic  18.4 us (4%)
  between operations  18 us (4%)
  matrix products  16 us (3%)
    psum x1, waiting for transfers between devices, per_device(): lax.psum(local_block, named_axis)  71.4 us
    psum x1, blocking collectives, per_device(): lax.psum(lax.psum(local_block, named_axis), row_axis)  62.2 us
    all_gather x1, waiting for transfers between devices, per_device(): lax.all_gather(conv_weight[0, 0], ('sy', 'sx'), axis=0, tiled=True)  57.8 us
    psum x1, waiting for transfers between devices, per_device(): lax.psum(lax.psum(local_block, named_axis), row_axis)  56.3 us
    all_to_all x2, blocking collectives, per_device(): lax.all_to_all(outgoing, 'sy', split_axis=0, concat_axis=0, tiled=True)  47.8 us
    ppermute x3, starting transfers between devices, from_behind(): return lax.ppermute(block, axis, route)  34.4 us
    all_to_all x1, blocking collectives, per_device(): lax.all_to_all(lax.all_to_all(outgoing, 'sy', split_axis=0, concat_axis=0...  19.7 us
    all_to_all x1, waiting for transfers between devices, per_device(): lax.all_to_all(lax.all_to_all(outgoing, 'sy', split_axis=0, concat_axis=0...  15 us
  transfers between devices with their start and end apart: 15, of which 9 were waited for; matrix products, arithmetic and copies ran while one was open for 5% of the time, Pallas kernels for 0%

profile of v1, /device:TPU:1, one launch (start us, length us, event | category | flops | bytes accessed | tf_op | source)
XLA Modules:
  0.0 499.0 jit_solution(12483775749994646203)
XLA Ops:
  7.2 1.5 copy.50
  8.8 0.7 reduce
  9.5 2.0 convert_reduce_fusion.1
  11.5 0.5 fusion.15
  12.0 3.8 fusion.20
  15.8 4.0 collective-permute-start
  19.9 1.3 collective-permute-start.1
  21.2 3.3 collective-permute-done.1
  24.5 4.0 collective-permute-start.2
  28.6 1.3 collective-permute-start.3
  29.9 4.2 collective-permute-done.3
  34.1 0.6 maximum_select_fusion
  34.6 1.0 slice_dynamic-update-slice_fusion.17
  35.7 1.3 slice_dynamic-update-slice_fusion.16
  37.0 1.3 slice_dynamic-update-slice_fusion.15
  38.3 1.0 slice_dynamic-update-slice_fusion.14
  39.3 1.3 slice_dynamic-update-slice_fusion.13
  40.6 1.3 slice_dynamic-update-slice_fusion.12
  41.9 1.0 slice_dynamic-update-slice_fusion.11
  42.9 1.4 slice_dynamic-update-slice_fusion.10
  44.3 1.3 slice_dynamic-update-slice_fusion.9
  45.5 57.8 %all-gather.3.cloned.1.call-done = bf16[1,1,3456,384]{3,1,0,2:T(2,128)(2,1)} async-done(((bf16[1,1,54,384]{3,1,0,2:T(2,128)(2,1)}), bf16[1,1,3456,384]{3,1,0,2:T(2,128)(2,1)}) %all-gather.3.cloned.1.call-update) | async-done | bytes 2654224 | tf_op jit(solution)/shard_map/all_gather | solution.py:81
  103.3 8.4 %fusion.22 = bf16[32,32,384]{2,1,0:T(8,128)(2,1)S(1)} fusion(bf16[32,32,384]{2,1,0:T(8,128)(2,1)S(1)} %get-tuple-element.14, bf16[32,32,3456]{2,1,0:T(8,128)(2,1)} %slice_dynamic-update-slice_fusion.9, bf16[1,1,3456,384]{3,1,0,2:T(2,128)(2,1)} %all-gather.3.cloned.1.call-done), kind=kOutput, calls=%fused_computation.30 | convolution fusion | flops 2719088640 | bytes 11304960 | tf_op jit(solution)/shard_map/dot_general | solution.py:79
  111.9 0.4 bitcast_select_fusion.2
  112.3 23.7 %all_to_all.20 = bf16[8,4,8,4,384]{4,3,1,2,0:T(4,128)(2,1)S(1)} all-to-all(bf16[8,4,8,4,384]{4,3,1,2,0:T(4,128)(2,1)S(1)} %bitcast_select_fusion.2), channel_id=1, replica_groups=mesh['section'=2,'sy'=8,'sx'=8,'mb'=4] {'sy'}, dimensions={0} | all-to-all | bytes 1572864 | tf_op jit(solution)/shard_map/all_to_all | solution.py:97
  136.3 19.7 %all_to_all.21 = bf16[8,4,8,4,384]{4,3,1,0,2:T(4,128)(2,1)S(1)} all-to-all(bf16[8,4,8,4,384]{4,3,1,0,2:T(4,128)(2,1)S(1)} %copy.53), channel_id=1, replica_groups=mesh['section'=2,'sy'=8,'sx'=8,'mb'=4] {'sx'}, dimensions={2} | all-to-all | bytes 1572864 | tf_op jit(solution)/shard_map/all_to_all | solution.py:96
  156.5 0.7 copy.55
  157.3 1.5 collective-permute-start.4
  158.8 9.2 %collective-permute-done.4 = bf16[32,32,384]{2,1,0:T(8,128)(2,1)S(1)} collective-permute-done((bf16[32,32,384]{2,1,0:T(8,128)(2,1)S(1)}, bf16[32,32,384]{2,1,0:T(8,128)(2,1)S(1)}, u32[]{:S(2)}, u32[]{:S(2)}) %collective-permute-start.4) | collective-permute-done | bytes 786464 | tf_op jit(solution)/shard_map/ppermute | solution.py:25
  168.2 0.5 fusion.8
  168.7 3.8 fusion.13
  172.6 1.4 collective-permute-start.5
  174.0 1.3 collective-permute-start.6
  175.3 3.3 collective-permute-done.6
  178.6 2.2 collective-permute-start.7
  180.8 1.3 collective-permute-start.8
  182.1 3.6 collective-permute-done.8
  185.7 0.6 maximum_select_fusion.1
  186.4 0.4 slice_dynamic-update-slice_fusion.7
  189.1 3.9 fusion.24
  193.1 0.4 bitcast_select_fusion.1
  193.6 24.2 %all_to_all.22 = bf16[8,4,8,4,384]{4,3,1,2,0:T(4,128)(2,1)S(1)} all-to-all(bf16[8,4,8,4,384]{4,3,1,2,0:T(4,128)(2,1)S(1)} %bitcast_select_fusion.1), channel_id=1, replica_groups=mesh['section'=2,'sy'=8,'sx'=8,'mb'=4] {'sy'}, dimensions={0} | all-to-all | bytes 1572864 | tf_op jit(solution)/shard_map/all_to_all | solution.py:97
  217.7 1.2 copy.58
  218.9 3.5 all-to-all-start.3
  222.8 1.1 bitcast_convert_fusion.1
  223.9 2.6 copy.63
  226.5 15.0 %all-to-all-done.3 = bf16[8,4,8,4,384]{4,3,1,0,2:T(4,128)(2,1)S(1)} async-done(((bf16[8,4,8,4,384]{4,3,1,0,2:T(4,128)(2,1)}), bf16[8,4,8,4,384]{4,3,1,0,2:T(4,128)(2,1)S(1)}, u32[]{:S(2)}, u32[]{:S(2)}) %all-to-all-start.3) | async-done | bytes 786464 | tf_op jit(solution)/shard_map/all_to_all | solution.py:96
  241.8 1.1 reshape.86
  242.9 0.7 copy.60
  243.6 0.4 copy-done.2
  244.2 1.0 copy-done.1
  245.3 0.5 fusion.58
  246.0 1.3 convolution_select_fusion
  247.4 71.4 %all-reduce.5.cloned.1.call-done = f32[384,256]{1,0:T(8,128)} async-done(((f32[384,256]{1,0:T(8,128)}), f32[384,256]{1,0:T(8,128)}) %all-reduce.5.cloned.1.call-update) | async-done | bytes 393232 | tf_op jit(solution)/shard_map/psum | solution.py:134
  318.8 0.6 subtract_reduce_fusion
  320.1 13.2 %psum.30 = f32[]{:T(128)} all-reduce(f32[]{:T(128)S(6)} %select_n.85), channel_id=1, replica_groups=mesh['section'=2,'sy'=8,'sx'=8,'mb'=4] {'sy'}, use_global_device_ids=true, to_apply=%region_11.12 | all-reduce | flops 1 | bytes 8 | tf_op jit(solution)/shard_map/psum | solution.py:134
  333.2 62.2 %psum.31 = f32[]{:T(128)} all-reduce(f32[]{:T(128)} %psum.30), channel_id=1, replica_groups=mesh['section'=2,'sy'=8,'sx'=8,'mb'=4] {'sx','mb'}, use_global_device_ids=true, to_apply=%region_12.13 | all-reduce | flops 1 | bytes 8 | tf_op jit(solution)/shard_map/psum | solution.py:133
  396.3 25.9 %collective-permute-start.10 = (bf16[]{:T(256)}, bf16[]{:T(256)}, u32[]{:S(2)}, u32[]{:S(2)}) collective-permute-start(bf16[]{:T(256)} %convert_element_type.60), channel_id=1, source_target_pairs={{256,0},{257,1},{258,2},{259,3},{260,4},{261,5},{262,6},{263,7},{2... | collective-permute-start | bytes 14 | tf_op jit(solution)/shard_map/ppermute | solution.py:25
  422.2 56.3 %all-reduce.7.cloned.1.call-done = f32[384,256]{1,0:T(8,128)} async-done(((f32[384,256]{1,0:T(8,128)}), f32[384,256]{1,0:T(8,128)}) %all-reduce.7.cloned.1.call-update) | async-done | bytes 393232 | tf_op jit(solution)/shard_map/psum | solution.py:133
  478.5 1.7 multiply_reduce_fusion
  480.9 1.0 broadcast_multiply_fusion
  482.0 7.0 %collective-permute-start.9 = (bf16[192,256]{1,0:T(8,128)(2,1)S(1)}, bf16[192,256]{1,0:T(8,128)(2,1)S(1)}, u32[]{:S(2)}, u32[]{:S(2)}) collective-permute-start(bf16[192,256]{1,0:T(8,128)(2,1)S(1)} %slice.157), channel_id=1, source_target_pairs={{256,0},{257,1},{258,2},{259,3},{260,4},{261,5},{262,6},{263,7},{2... | collective-permute-start | bytes 294920 | tf_op jit(solution)/shard_map/ppermute | solution.py:25
  489.0 1.0 select_bitcast_fusion
  490.7 0.7 slice_select_fusion
  (56 shorter events, 5.4 us)
Async XLA Ops:
  7.2 2.3 copy-start
  7.2 96.1 %all-gather.3.cloned.1.call-start = ((), (), s32[]{:S(2)}) async-start(), calls=%async_computation.6 | async-start | bytes 5391360 | tf_op jit(solution)/shard_map/all_gather | solution.py:81
  15.8 5.3 %collective-permute-start = (bf16[1,32,384]{2,1,0:T(8,128)(2,1)S(1)}, bf16[1,32,384]{2,1,0:T(8,128)(2,1)S(1)}, u32[]{:S(2)}, u32[]{:S(2)}) collective-permute-start(bf16[1,32,384]{2,1,0:T(8,128)(2,1)S(1)} %get-tuple-element.11), channel_id=1, source_target_pairs={{0,32},{32,64},{64,96},{96,128},{128,160},{160,192},{192,224},{1,3... | collective-permute-start | bytes 73736 | tf_op jit(solution)/shard_map/ppermute | solution.py:14
  19.9 4.6 collective-permute-start.1
  24.5 5.3 %collective-permute-start.2 = (bf16[34,1,384]{2,1,0:T(2,128)(2,1)S(1)}, bf16[34,1,384]{2,1,0:T(2,128)(2,1)S(1)}, u32[]{:S(2)}, u32[]{:S(2)}) collective-permute-start(bf16[34,1,384]{2,1,0:T(2,128)(2,1)S(1)} %get-tuple-element.7), channel_id=1, source_target_pairs={{0,4},{4,8},{8,12},{12,16},{16,20},{20,24},{24,28},{1,5},{5,9},{9,... | collective-permute-start | bytes 78344 | tf_op jit(solution)/shard_map/ppermute | solution.py:14
  28.6 5.5 %collective-permute-start.3 = (bf16[34,1,384]{2,1,0:T(2,128)(2,1)S(1)}, bf16[34,1,384]{2,1,0:T(2,128)(2,1)S(1)}, u32[]{:S(2)}, u32[]{:S(2)}) collective-permute-start(bf16[34,1,384]{2,1,0:T(2,128)(2,1)S(1)} %get-tuple-element.8), channel_id=1, source_target_pairs={{4,0},{8,4},{12,8},{16,12},{20,16},{24,20},{28,24},{5,1},{9,5},{13... | collective-permute-start | bytes 78344 | tf_op jit(solution)/shard_map/ppermute | solution.py:17
  157.3 10.7 %collective-permute-start.4 = (bf16[32,32,384]{2,1,0:T(8,128)(2,1)S(1)}, bf16[32,32,384]{2,1,0:T(8,128)(2,1)S(1)}, u32[]{:S(2)}, u32[]{:S(2)}) collective-permute-start(bf16[32,32,384]{2,1,0:T(8,128)(2,1)S(1)} %broadcast_select_fusion), channel_id=1, source_target_pairs={{0,256},{1,257},{2,258},{3,259},{4,260},{5,261},{6,262},{7,263},{8... | collective-permute-start | bytes 2359304 | tf_op jit(solution)/shard_map/ppermute | solution.py:25
  172.6 2.7 collective-permute-start.5
  174.0 4.6 collective-permute-start.6
  178.6 3.5 collective-permute-start.7
  180.8 4.9 collective-permute-start.8
  186.3 2.8 slice-start
  187.3 1.7 slice-start.1
  217.7 5.0 %copy-start.3 = (bf16[1,32,32,256]{3,2,1,0:T(8,128)(2,1)S(1)}, bf16[1,32,32,256]{3,2,1,0:T(8,128)(2,1)}, u32[]{:S(2)}) copy-start(bf16[1,32,32,256]{3,2,1,0:T(8,128)(2,1)} %param.12) | copy-start | bytes 1572868
  218.9 22.6 %all-to-all-start.3 = ((bf16[8,4,8,4,384]{4,3,1,0,2:T(4,128)(2,1)}), bf16[8,4,8,4,384]{4,3,1,0,2:T(4,128)(2,1)S(1)}, u32[]{:S(2)}, u32[]{:S(2)}) async-start(bf16[8,4,8,4,384]{4,3,1,0,2:T(4,128)(2,1)} %copy.58), calls=%async_computation.3 | async-start | bytes 1572864 | tf_op jit(solution)/shard_map/all_to_all | solution.py:96
  222.5 4.0 copy-start.5
  222.5 96.3 %all-reduce.5.cloned.1.call-start = ((), (), s32[]{:S(2)}) async-start(), calls=%async_computation.4 | async-start | bytes 786432 | tf_op jit(solution)/shard_map/psum | solution.py:134
  242.9 1.1 copy-start.2
  244.0 1.2 copy-start.1
  244.0 1.2 copy-start.4
  247.4 231.2 %all-reduce.7.cloned.1.call-start = ((), (), s32[]{:S(2)}) async-start(), calls=%async_computation.5 | async-start | bytes 786432 | tf_op jit(solution)/shard_map/psum | solution.py:133
  396.3 93.7 %collective-permute-start.10 = (bf16[]{:T(256)}, bf16[]{:T(256)}, u32[]{:S(2)}, u32[]{:S(2)}) collective-permute-start(bf16[]{:T(256)} %convert_element_type.60), channel_id=1, source_target_pairs={{256,0},{257,1},{258,2},{259,3},{260,4},{261,5},{262,6},{263,7},{2... | collective-permute-start | bytes 14 | tf_op jit(solution)/shard_map/ppermute | solution.py:25
  482.0 8.7 %collective-permute-start.9 = (bf16[192,256]{1,0:T(8,128)(2,1)S(1)}, bf16[192,256]{1,0:T(8,128)(2,1)S(1)}, u32[]{:S(2)}, u32[]{:S(2)}) collective-permute-start(bf16[192,256]{1,0:T(8,128)(2,1)S(1)} %slice.157), channel_id=1, source_target_pairs={{256,0},{257,1},{258,2},{259,3},{260,4},{261,5},{262,6},{263,7},{2... | collective-permute-start | bytes 294920 | tf_op jit(solution)/shard_map/ppermute | solution.py:25
Sparse Core Ops, SparseCore 0:
  11.7 91.6 all-gather.2
  247.5 71.2 all-reduce.4
  322.6 155.9 all-reduce.6
